TPU v7x, 512 devices: a whole 4x8x8 slice. The times are simulated.
512 devices in a mesh: row: 32 (over y, x_hi, core), col: 16 (over z, x_lo).
Axes of the slice: x: 4 (x_hi: 2, x_lo: 2; x = x_hi * 2 + x_lo), y: 8, z: 8, core: 2. Of those that a mesh axis runs over, the one named last changes fastest.
Arguments:
- features: bfloat16 [65536, 512], P(('col', 'row')), may hold values from -6 to 6
- block_values: bfloat16 [32, 16, 12, 128, 128], P('row', 'col'), may hold values from -0.21875 to 0.21875
- block_rows: int32 [32, 16, 12], P('row', 'col'), may hold values from 0 to 15
- block_cols: int32 [32, 16, 12], P('row', 'col'), may hold values from 0 to 31
- block_count: int32 [32, 16], P('row', 'col'), may hold values from 3 to 12, as said below
- weight: bfloat16 [512, 512], replicated, may hold values from -0.25 to 0.25
- bias: float32 [512], replicated, may hold values from -3 to 3
- cotangent: bfloat16 [65536, 512], P(('row', 'col')), may hold values from -6 to 6
Outputs:
- hidden: bfloat16 [65536, 512], P(('row', 'col'))
- weight_grad: float32 [512, 512], replicated
- bias_grad: float32 [512], replicated
- feature_grad: bfloat16 [65536, 512], P(('col', 'row'))
Inputs may be any that keep to these rules, and one draw needn't show every extreme that they name: `block_count`: no grid tile has more than 12 live slots, and some tile has exactly 12.
All inputs are finite; a program needn't handle non-finite values.
Results may differ from a plain program's by a relative error of at most 0.017.
Values may be sent and summed in bfloat16 or wider, within the bound.
A program may use at most 64 MiB of HBM per device.

v0:
```python
import jax
import jax.numpy as jnp
from jax import lax
from jax.sharding import PartitionSpec as P


def slot_product(tile_values, tile_rows, tile_cols, live_count, source, out_len, backward):
    capacity = tile_values.shape[0]
    block_size = tile_values.shape[1]
    width = source.shape[1]
    group = max([d for d in range(1, min(capacity, 16) + 1) if capacity % d == 0])
    groups = capacity // group
    panels = source.reshape(source.shape[0] // block_size, block_size, width)
    out_blocks = out_len // block_size
    if backward:
        source_ids = tile_rows
        target_ids = tile_cols
        form = "sba,sbf->saf"
    else:
        source_ids = tile_cols
        target_ids = tile_rows
        form = "sab,sbf->saf"
    alive = jnp.arange(capacity, dtype=jnp.int32) < live_count
    places = jnp.arange(out_blocks, dtype=jnp.int32)

    def one_group(total, items):
        values_part, source_part, target_part, alive_part = items
        segments = jnp.take(panels, source_part, axis=0)
        products = jnp.einsum(form, values_part, segments, preferred_element_type=jnp.float32)
        selector = ((target_part[None, :] == places[:, None]) & alive_part[None, :]).astype(
            jnp.float32
        )
        added = jnp.einsum("rs,saf->raf", selector, products, precision=lax.Precision.HIGHEST)
        return (total + added, None)

    items = (
        tile_values.reshape(groups, group, block_size, block_size),
        source_ids.reshape(groups, group),
        target_ids.reshape(groups, group),
        alive.reshape(groups, group),
    )
    start = jnp.zeros((out_blocks, block_size, width), jnp.float32)
    total, _ = lax.scan(one_group, start, items)
    return total.reshape(out_len, width)


def global_grads(local_weight, local_bias):
    return lax.psum((local_weight, local_bias), ("row", "col"))


def transposed_product(left, weight):
    return lax.dot_general(
        left, weight, (((1,), (1,)), ((), ())), preferred_element_type=jnp.float32
    ).astype(jnp.bfloat16)


def source_total(received):
    return jnp.sum(received.astype(jnp.float32), axis=0).astype(jnp.bfloat16)


def per_device(
    features, block_values, block_rows, block_cols, block_count, weight, bias, cotangent
):
    tile_values = block_values[0, 0]
    tile_rows = block_rows[0, 0]
    tile_cols = block_cols[0, 0]
    live_count = block_count[0, 0]
    own_nodes = features.shape[0]
    width = features.shape[1]
    row_len = lax.axis_size("col") * own_nodes
    gathered = lax.all_gather(features, "row", axis=0, tiled=True)
    col_len = gathered.shape[0]
    partial_value = slot_product(
        tile_values, tile_rows, tile_cols, live_count, gathered, row_len, False
    )
    aggregate = lax.psum_scatter(
        partial_value.astype(jnp.bfloat16), "col", scatter_dimension=0, tiled=True
    )
    preact = jnp.dot(aggregate, weight, preferred_element_type=jnp.float32) + bias
    hidden = jax.nn.silu(preact).astype(jnp.bfloat16)
    sigma = jax.nn.sigmoid(preact)
    grad_pre = cotangent.astype(jnp.float32) * sigma * (1.0 + preact * (1.0 - sigma))
    grad_low = grad_pre.astype(jnp.bfloat16)
    local_weight = lax.dot_general(
        aggregate, grad_low, (((0,), (0,)), ((), ())), preferred_element_type=jnp.float32
    )
    local_bias = jnp.sum(grad_pre, axis=0)
    grad_agg = transposed_product(grad_low, weight)
    grad_panel = lax.all_gather(grad_agg, "col", axis=0, tiled=True)
    back = slot_product(tile_values, tile_rows, tile_cols, live_count, grad_panel, col_len, True)
    back_low = back.astype(jnp.bfloat16).reshape(col_len // own_nodes, own_nodes, width)
    received = lax.all_to_all(back_low, "row", split_axis=0, concat_axis=0, tiled=True)
    feature_grad = source_total(received)
    weight_grad, bias_grad = global_grads(local_weight, local_bias)
    return (hidden, weight_grad, bias_grad, feature_grad)


def solution(mesh):
    in_specs = (
        P(("col", "row"), None),
        P("row", "col", None, None, None),
        P("row", "col", None),
        P("row", "col", None),
        P("row", "col"),
        P(),
        P(),
        P(("row", "col"), None),
    )
    out_specs = (P(("row", "col"), None), P(), P(), P(("col", "row"), None))
    return jax.shard_map(
        per_device, mesh=mesh, in_specs=in_specs, out_specs=out_specs, check_vma=False
    )
```

profile of v0, /device:TPU:24, one launch (start us, length us, event | category | flops | bytes accessed | tf_op | source)
XLA Modules:
  0.0 616.6 jit_solution(6726816917784381716)
XLA Ops:
  7.2 0.0 copy-start
  7.2 0.0 all-gather.3.cloned.1.call-start
  7.2 0.7 all-gather.3.cloned.1.call-update
  7.9 0.0 reduce-scatter.2.cloned.1.call-start
  8.6 0.7 fusion.21
  9.3 0.7 compare_and_fusion.1
  10.0 97.7 %all-gather.3.cloned.1.call-done = bf16[4096,512]{1,0:T(8,128)(2,1)} async-done(((bf16[128,512]{1,0:T(8,128)(2,1)}), bf16[4096,512]{1,0:T(8,128)(2,1)}) %all-gather.3.cloned.1.call-update) | async-done | bytes 4194320 | tf_op jit(solution)/shard_map/all_gather | solution.py:71
  107.6 2.8 gather_fusion
  110.5 2.4 convolution_bitcast_fusion.1
  112.9 5.2 copy.18
  118.1 4.3 convolution_convert_fusion.1
  122.5 2.5 copy.19
  125.0 0.0 reduce-scatter.2.cloned.1.call-update
  125.0 0.0 all-gather.5.cloned.1.call-start
  125.1 76.2 %reduce-scatter.2.cloned.1.call-done = bf16[128,512]{1,0:T(8,128)(2,1)} async-done(((bf16[2048,512]{1,0:T(8,128)(2,1)}), bf16[128,512]{1,0:T(8,128)(2,1)}) %reduce-scatter.2.cloned.1.call-update) | async-done | bytes 131088 | tf_op jit(solution)/shard_map/reduce_scatter | solution.py:76
  201.3 1.9 fusion.25
  203.2 1.0 convolution_convert_fusion.2
  204.2 0.0 all-gather.5.cloned.1.call-update
  204.2 74.5 %all-gather.5.cloned.1.call-done = bf16[2048,512]{1,0:T(8,128)(2,1)} async-done(((bf16[128,512]{1,0:T(8,128)(2,1)}), bf16[2048,512]{1,0:T(8,128)(2,1)}) %all-gather.5.cloned.1.call-update) | async-done | bytes 2097168 | tf_op jit(solution)/shard_map/all_gather | solution.py:89
  278.8 2.2 gather_fusion.1
  281.0 2.4 convolution_bitcast_fusion
  283.4 5.2 copy.21
  288.6 5.5 convolution_convert_fusion
  294.2 4.4 copy.22
  298.5 9.7 %all-to-all-start = ((bf16[32,128,512]{2,1,0:T(8,128)(2,1)}), bf16[32,128,512]{2,1,0:T(8,128)(2,1)}, u32[]{:S(2)}, u32[]{:S(2)}) async-start(bf16[32,128,512]{2,1,0:T(8,128)(2,1)} %copy.22), calls=%async_computation.1 | async-start | bytes 8388608 | tf_op jit(solution)/shard_map/all_to_all | solution.py:92
  308.2 0.0 all-reduce.2.cloned.1.call-start
  308.3 1.3 fusion.9
  309.6 0.0 all-reduce.2.cloned.1.call-update
  309.6 183.3 %psum.15 = f32[512]{0:T(512)} all-reduce(f32[512]{0:T(512)S(1)} %get-tuple-element.36), channel_id=1, replica_groups=mesh['row'=32,'col'=16] {'row','col'}, use_global_device_ids=true, to_apply=%region_3.4 | all-reduce | flops 512 | bytes 4096 | tf_op jit(solution)/shard_map/psum | solution.py:48
  492.9 3.5 reduce_sum.22
  496.4 111.4 %all-reduce.2.cloned.1.call-done = f32[512,512]{1,0:T(8,128)} async-done(((f32[512,512]{1,0:T(8,128)}), f32[512,512]{1,0:T(8,128)}) %all-reduce.2.cloned.1.call-update) | async-done | bytes 1048592 | tf_op jit(solution)/shard_map/psum | solution.py:48
  607.8 2.3 copy.27
  (19 shorter events, 0.1 us)
Async XLA Ops:
  7.2 194.1 %copy-start = (bf16[512,512]{1,0:T(8,128)(2,1)S(1)}, bf16[512,512]{1,0:T(8,128)(2,1)}, u32[]{:S(2)}) copy-start(bf16[512,512]{1,0:T(8,128)(2,1)} %param.13) | copy-start | bytes 1572868
  7.2 103.3 %copy-start.1 = (bf16[1,1,12,128,128]{4,3,2,1,0:T(8,128)(2,1)S(1)}, bf16[1,1,12,128,128]{4,3,2,1,0:T(8,128)(2,1)}, u32[]{:S(2)}) copy-start(bf16[1,1,12,128,128]{4,3,2,1,0:T(8,128)(2,1)} %param.9) | copy-start | bytes 1179652
  7.2 100.5 %all-gather.3.cloned.1.call-start = ((), (), s32[]{:S(2)}) async-start(), calls=%async_computation.2 | async-start | bytes 4325376 | tf_op jit(solution)/shard_map/all_gather | solution.py:71
  7.9 193.4 %reduce-scatter.2.cloned.1.call-start = ((), (), s32[]{:S(2)}) async-start(), calls=%async_computation.3 | async-start | bytes 2228224 | tf_op jit(solution)/shard_map/reduce_scatter | solution.py:76
  112.9 5.3 copy-start.4
  125.0 76.3 %copy-start.5 = (bf16[128,512]{1,0:T(8,128)(2,1)S(1)}, bf16[128,512]{1,0:T(8,128)(2,1)}, u32[]{:S(2)}) copy-start(bf16[128,512]{1,0:T(8,128)(2,1)} %param.15) | copy-start | bytes 393220
  125.0 76.3 %copy-start.6 = (f32[512]{0:T(512)S(1)}, f32[512]{0:T(512)}, u32[]{:S(2)}) copy-start(f32[512]{0:T(512)} %param.14) | copy-start | bytes 6148
  125.0 153.8 %all-gather.5.cloned.1.call-start = ((), (), s32[]{:S(2)}) async-start(), calls=%async_computation.5 | async-start | bytes 2228224 | tf_op jit(solution)/shard_map/all_gather | solution.py:89
  283.4 5.3 copy-start.3
  298.5 9.7 %copy-start.2 = (bf16[128,512]{1,0:T(8,128)(2,1)S(1)}, bf16[128,512]{1,0:T(8,128)(2,1)}, u32[]{:S(2)}) copy-start(bf16[128,512]{1,0:T(8,128)(2,1)} %reduce-scatter.2.cloned.1.call-done) | copy-start | bytes 393220
  298.5 194.4 %all-to-all-start = ((bf16[32,128,512]{2,1,0:T(8,128)(2,1)}), bf16[32,128,512]{2,1,0:T(8,128)(2,1)}, u32[]{:S(2)}, u32[]{:S(2)}) async-start(bf16[32,128,512]{2,1,0:T(8,128)(2,1)} %copy.22), calls=%async_computation.1 | async-start | bytes 8388608 | tf_op jit(solution)/shard_map/all_to_all | solution.py:92
  308.2 299.5 %all-reduce.2.cloned.1.call-start = ((), (), s32[]{:S(2)}) async-start(), calls=%async_computation.4 | async-start | bytes 2097152 | tf_op jit(solution)/shard_map/psum | solution.py:48
Sparse Core Ops, SparseCore 0:
  11.4 96.2 all-gather.2
  125.1 76.1 reduce-scatter.1
  204.3 74.4 all-gather.4
  314.4 293.3 all-reduce.1
where the time goes:
time: 617 us
  waiting for transfers between devices  361 us (59%)
  blocking collectives  183 us (30%)
  local copies, waits for them, and re-layouts  24.8 us (4%)
  matrix products  18.8 us (3%)
  between operations  14.5 us (2%)
  starting transfers between devices  9.84 us (2%)
    psum x1, blocking collectives, global_grads(): return lax.psum((local_weight, local_bias), ('row', 'col'))  183 us
    psum x1, waiting for transfers between devices, global_grads(): return lax.psum((local_weight, local_bias), ('row', 'col'))  111 us
    all_gather x1, waiting for transfers between devices, per_device(): gathered = lax.all_gather(features, 'row', axis=0, tiled=True)  97.7 us
    reduce_scatter x1, waiting for transfers between devices, per_device(): lax.psum_scatter(partial_value.astype(jnp.bfloat16), 'col', scatter_dimen...  76.2 us
    all_gather x1, waiting for transfers between devices, per_device(): grad_panel = lax.all_gather(grad_agg, 'col', axis=0, tiled=True)  74.5 us
  transfers between devices with their start and end apart: 5, of which 4 were waited for; matrix products, arithmetic and copies ran while one was open for 1% of the time, Pallas kernels for 0%

commit v1 on v0

--- a/solution.py
+++ b/solution.py
@@ -45,7 +45,7 @@
 
 
 def global_grads(local_weight, local_bias):
-    return lax.psum((local_weight, local_bias), ("row", "col"))
+    return lax.psum(lax.psum((local_weight, local_bias), "row"), "col")
 
 
 def transposed_product(left, weight):

time: 617 us -> 764 us (1.24)
  the two profiles are of different devices: /device:TPU:24 before, /device:TPU:8 now
where the time goes in v1:
time: 764 us
  waiting for transfers between devices  587 us (77%)
  blocking collectives  104 us (14%)
  local copies, waits for them, and re-layouts  24.7 us (3%)
  matrix products  18.8 us (2%)
  between operations  14.5 us (2%)
  starting transfers between devices  10.1 us (1%)
    psum x2, waiting for transfers between devices, global_grads(): return lax.psum(lax.psum((local_weight, local_bias), 'row'), 'col')  338 us
    psum x2, blocking collectives, global_grads(): return lax.psum(lax.psum((local_weight, local_bias), 'row'), 'col')  104 us
    all_gather x1, waiting for transfers between devices, per_device(): gathered = lax.all_gather(features, 'row', axis=0, tiled=True)  97.8 us
    reduce_scatter x1, waiting for transfers between devices, per_device(): lax.psum_scatter(partial_value.astype(jnp.bfloat16), 'col', scatter_dimen...  76.2 us
    all_gather x1, waiting for transfers between devices, per_device(): grad_panel = lax.all_gather(grad_agg, 'col', axis=0, tiled=True)  74.3 us
  transfers between devices with their start and end apart: 6, of which 5 were waited for; matrix products, arithmetic and copies ran while one was open for 1% of the time, Pallas kernels for 0%

profile of v1, /device:TPU:8, one launch (start us, length us, event | category | flops | bytes accessed | tf_op | source)
XLA Modules:
  0.0 763.7 jit_solution(12115475459545178392)
XLA Ops:
  7.2 0.0 all-gather.3.cloned.1.call-start
  7.2 0.7 all-gather.3.cloned.1.call-update
  7.9 0.0 reduce-scatter.2.cloned.1.call-start
  8.6 0.7 fusion.21
  9.3 0.7 compare_and_fusion.1
  10.0 97.8 %all-gather.3.cloned.1.call-done = bf16[4096,512]{1,0:T(8,128)(2,1)} async-done(((bf16[128,512]{1,0:T(8,128)(2,1)}), bf16[4096,512]{1,0:T(8,128)(2,1)}) %all-gather.3.cloned.1.call-update) | async-done | bytes 4194320 | tf_op jit(solution)/shard_map/all_gather | solution.py:71
  107.8 2.8 gather_fusion
  110.6 2.4 convolution_bitcast_fusion.1
  113.0 5.3 copy.18
  118.3 4.3 convolution_convert_fusion.1
  122.6 2.5 copy.19
  125.1 0.0 reduce-scatter.2.cloned.1.call-update
  125.1 0.0 all-gather.5.cloned.1.call-start
  125.2 76.2 %reduce-scatter.2.cloned.1.call-done = bf16[128,512]{1,0:T(8,128)(2,1)} async-done(((bf16[2048,512]{1,0:T(8,128)(2,1)}), bf16[128,512]{1,0:T(8,128)(2,1)}) %reduce-scatter.2.cloned.1.call-update) | async-done | bytes 131088 | tf_op jit(solution)/shard_map/reduce_scatter | solution.py:76
  201.4 1.9 fusion.25
  203.3 1.0 convolution_convert_fusion.2
  204.3 74.3 %all-gather.5.cloned.1.call-done = bf16[2048,512]{1,0:T(8,128)(2,1)} async-done(((bf16[128,512]{1,0:T(8,128)(2,1)}), bf16[2048,512]{1,0:T(8,128)(2,1)}) %all-gather.5.cloned.1.call-update) | async-done | bytes 2097168 | tf_op jit(solution)/shard_map/all_gather | solution.py:89
  278.6 2.2 gather_fusion.1
  280.9 2.4 convolution_bitcast_fusion
  283.3 5.3 copy.21
  288.5 5.5 convolution_convert_fusion
  294.0 4.4 copy.22
  298.4 9.9 %all-to-all-start = ((bf16[32,128,512]{2,1,0:T(8,128)(2,1)}), bf16[32,128,512]{2,1,0:T(8,128)(2,1)}, u32[]{:S(2)}, u32[]{:S(2)}) async-start(bf16[32,128,512]{2,1,0:T(8,128)(2,1)} %copy.22), calls=%async_computation.1 | async-start | bytes 8388608 | tf_op jit(solution)/shard_map/all_to_all | solution.py:92
  308.3 0.0 all-reduce.3.cloned.1.call-start
  308.4 1.3 fusion.9
  309.7 0.0 all-reduce.5.cloned.1.call-start
  309.7 290.5 %all-reduce.3.cloned.1.call-done = f32[512,512]{1,0:T(8,128)} async-done(((f32[512,512]{1,0:T(8,128)}), f32[512,512]{1,0:T(8,128)}) %all-reduce.3.cloned.1.call-update) | async-done | bytes 1048592 | tf_op jit(solution)/shard_map/psum | solution.py:48
  600.3 68.4 %psum.30 = f32[512]{0:T(512)S(1)} all-reduce(f32[512]{0:T(512)S(1)} %get-tuple-element.36), channel_id=1, replica_groups=mesh['row'=32,'col'=16] {'row'}, use_global_device_ids=true, to_apply=%region_4.5 | all-reduce | flops 512 | bytes 4096 | tf_op jit(solution)/shard_map/psum | solution.py:48
  668.7 35.2 %psum.31 = f32[512]{0:T(512)} all-reduce(f32[512]{0:T(512)S(1)} %psum.30), channel_id=1, replica_groups=mesh['row'=32,'col'=16] {'col'}, use_global_device_ids=true, to_apply=%region_5.6 | all-reduce | flops 512 | bytes 4096 | tf_op jit(solution)/shard_map/psum | solution.py:48
  703.9 3.5 reduce_sum.22
  707.4 47.6 %all-reduce.5.cloned.1.call-done = f32[512,512]{1,0:T(8,128)} async-done(((f32[512,512]{1,0:T(8,128)}), f32[512,512]{1,0:T(8,128)}) %all-reduce.5.cloned.1.call-update) | async-done | bytes 1048592 | tf_op jit(solution)/shard_map/psum | solution.py:48
  755.0 2.3 copy.28
  (23 shorter events, 0.1 us)
Async XLA Ops:
  7.2 194.2 %copy-start = (bf16[512,512]{1,0:T(8,128)(2,1)S(1)}, bf16[512,512]{1,0:T(8,128)(2,1)}, u32[]{:S(2)}) copy-start(bf16[512,512]{1,0:T(8,128)(2,1)} %param.13) | copy-start | bytes 1572868
  7.2 103.4 %copy-start.1 = (bf16[1,1,12,128,128]{4,3,2,1,0:T(8,128)(2,1)S(1)}, bf16[1,1,12,128,128]{4,3,2,1,0:T(8,128)(2,1)}, u32[]{:S(2)}) copy-start(bf16[1,1,12,128,128]{4,3,2,1,0:T(8,128)(2,1)} %param.9) | copy-start | bytes 1179652
  7.2 100.6 %all-gather.3.cloned.1.call-start = ((), (), s32[]{:S(2)}) async-start(), calls=%async_computation.2 | async-start | bytes 4325376 | tf_op jit(solution)/shard_map/all_gather | solution.py:71
  7.9 193.4 %reduce-scatter.2.cloned.1.call-start = ((), (), s32[]{:S(2)}) async-start(), calls=%async_computation.3 | async-start | bytes 2228224 | tf_op jit(solution)/shard_map/reduce_scatter | solution.py:76
  113.0 5.3 copy-start.4
  125.1 76.3 %copy-start.5 = (bf16[128,512]{1,0:T(8,128)(2,1)S(1)}, bf16[128,512]{1,0:T(8,128)(2,1)}, u32[]{:S(2)}) copy-start(bf16[128,512]{1,0:T(8,128)(2,1)} %param.15) | copy-start | bytes 393220
  125.1 76.3 %copy-start.6 = (f32[512]{0:T(512)S(1)}, f32[512]{0:T(512)}, u32[]{:S(2)}) copy-start(f32[512]{0:T(512)} %param.14) | copy-start | bytes 6148
  125.1 153.5 %all-gather.5.cloned.1.call-start = ((), (), s32[]{:S(2)}) async-start(), calls=%async_computation.6 | async-start | bytes 2228224 | tf_op jit(solution)/shard_map/all_gather | solution.py:89
  283.3 5.3 copy-start.3
  298.4 10.0 %copy-start.2 = (bf16[128,512]{1,0:T(8,128)(2,1)S(1)}, bf16[128,512]{1,0:T(8,128)(2,1)}, u32[]{:S(2)}) copy-start(bf16[128,512]{1,0:T(8,128)(2,1)} %reduce-scatter.2.cloned.1.call-done) | copy-start | bytes 393220
  298.4 405.5 %all-to-all-start = ((bf16[32,128,512]{2,1,0:T(8,128)(2,1)}), bf16[32,128,512]{2,1,0:T(8,128)(2,1)}, u32[]{:S(2)}, u32[]{:S(2)}) async-start(bf16[32,128,512]{2,1,0:T(8,128)(2,1)} %copy.22), calls=%async_computation.1 | async-start | bytes 8388608 | tf_op jit(solution)/shard_map/all_to_all | solution.py:92
  308.3 291.9 %all-reduce.3.cloned.1.call-start = ((), (), s32[]{:S(2)}) async-start(), calls=%async_computation.4 | async-start | bytes 2097152 | tf_op jit(solution)/shard_map/psum | solution.py:48
  309.7 445.3 %all-reduce.5.cloned.1.call-start = ((), (), s32[]{:S(2)}) async-start(), calls=%async_computation.5 | async-start | bytes 2097152 | tf_op jit(solution)/shard_map/psum | solution.py:48
Sparse Core Ops, SparseCore 0:
  11.4 96.3 all-gather.2
  125.3 76.0 reduce-scatter.1
  204.4 74.1 all-gather.4
  312.3 287.8 all-reduce.2
  603.3 151.6 all-reduce.4
